TPU v7x, 32 devices: a whole 2x2x4 slice. The times are simulated.
32 devices in a mesh: row: 8 (over y, x, core), col: 4 (over z).
Axes of the slice: x: 2, y: 2, z: 4, core: 2. Of those that a mesh axis runs over, the one named last changes fastest.
Arguments:
- built: bfloat16 [4096, 4096], P('row', 'col'), may hold values from -0.59765625 to 0.59765625
- build_order: int32 [32], replicated, may hold values from 0 to 31, each once
- p_pattern: int32 [32, 32], replicated, may hold values from 0 to 1, as said below
- q_pattern: int32 [32, 32], replicated, may hold values from 0 to 1, as said below
Outputs:
- purified: bfloat16 [4096, 4096], P('row', 'col')
Inputs may be any that keep to these rules, and one draw needn't show every extreme that they name: p_pattern is symmetric and 1 on the diagonal; p_pattern[i, j] is 0 unless the distance of i and j counted round the 32 blocks, or that of i and j + 16, is at most 1. q_pattern[i, j] is 0 unless the distance of i and j counted round the 32 blocks, or that of i and j + 16, is at most 2.
All inputs are finite; a program needn't handle non-finite values.
Results may differ from a plain program's by a relative error of at most 0.0045.
Values may be sent and summed in bfloat16 or wider, within the bound.
A program may use at most 128 MiB of HBM per device.

v0:
```python
import jax
import jax.numpy as jnp
from jax import lax
from jax.sharding import PartitionSpec as P

BS = 128


def contract(col_panel, portion):
    return jnp.dot(portion, col_panel, preferred_element_type=jnp.float32)


def body(built, build_order, p_pattern, q_pattern):
    row_count = built.shape[0] // BS
    col_count = built.shape[1] // BS
    block_count = build_order.shape[0]
    row_index = lax.axis_index("row")
    col_index = lax.axis_index("col")
    build_slab = lax.all_gather(built, "row", axis=0, tiled=True)
    blocks = build_slab.reshape(block_count, BS, col_count * BS)
    inverse = (
        jnp.zeros((block_count,), jnp.int32)
        .at[build_order]
        .set(jnp.arange(block_count, dtype=jnp.int32))
    )
    col_mask = lax.dynamic_slice_in_dim(p_pattern, col_index * col_count, col_count, 1).astype(
        jnp.bfloat16
    )
    ordered = blocks[inverse].reshape(block_count, BS, col_count, BS)
    columns = (ordered * col_mask[:, None, :, None]).reshape(block_count * BS, col_count * BS)
    start_block = row_index * row_count
    local_tile = lax.dynamic_slice_in_dim(columns, start_block * BS, row_count * BS, 0)
    q_block = lax.dynamic_slice(
        q_pattern, (start_block, col_index * col_count), (row_count, col_count)
    ).astype(jnp.float32)
    q_tile = jnp.broadcast_to(q_block[:, None, :, None], (row_count, BS, col_count, BS)).reshape(
        row_count * BS, col_count * BS
    )
    square = contract(columns, lax.all_gather(local_tile, "col", axis=1, tiled=True)) * q_tile
    rounded = square.astype(jnp.bfloat16)
    cubed_term = contract(columns, lax.all_gather(rounded, "col", axis=1, tiled=True))
    return ((3.0 * square - 2.0 * cubed_term) * q_tile).astype(jnp.bfloat16)


def solution(mesh):
    placed = (P("row", "col"), P(), P(), P())
    return jax.shard_map(
        body, mesh=mesh, in_specs=placed, out_specs=P("row", "col"), check_vma=False
    )
```

profile of v0, /device:TPU:0, one launch (start us, length us, event | category | flops | bytes accessed | tf_op | source)
XLA Modules:
  0.0 273.1 jit_solution(3212071331895305885)
XLA Ops:
  6.5 0.0 all-gather.4.cloned.1.call-start
  6.5 0.7 all-gather.4.cloned.1.call-update
  7.3 0.0 all-gather.6.cloned.1.call-start
  7.3 0.7 compare_select_fusion.1
  8.0 0.7 scatter_custom_fusion
  8.7 0.8 dynamic-slice_convert_fusion
  9.5 56.8 %all-gather.4.cloned.1.call-done = bf16[4096,1024]{1,0:T(8,128)(2,1)} async-done(((bf16[512,1024]{1,0:T(8,128)(2,1)}), bf16[4096,1024]{1,0:T(8,128)(2,1)}) %all-gather.4.cloned.1.call-update) | async-done | bytes 8388624 | tf_op jit(solution)/shard_map/all_gather | solution.py:19
  66.2 8.4 %gather_fusion = bf16[32,128,1024]{2,1,0:T(8,128)(2,1)} fusion(bf16[32,128,1024]{2,1,0:T(8,128)(2,1)} %bitcast.23, s32[1024]{0:T(1024)S(1)} %pad_clamp_fusion), kind=kCustom, calls=%fused_computation | custom fusion | bytes 16777344 | tf_op jit(solution)/shard_map/gather | solution.py:29
  74.6 0.0 copy-start
  74.7 1.1 mul.40
  75.8 2.2 copy-done
  78.0 1.9 bitcast_multiply_fusion
  79.9 0.0 copy-start.1
  80.0 3.2 %copy-done.1 = bf16[4096,1024]{1,0:T(8,128)(2,1)} copy-done((bf16[4096,1024]{1,0:T(8,128)(2,1)}, bf16[4096,1024]{1,0:T(8,128)(2,1)S(1)}, u32[]{:S(2)}) %copy-start.1) | copy-done | bytes 8388632
  83.2 1.0 constant_dynamic-slice_fusion
  84.2 0.0 all-gather.6.cloned.1.call-update
  84.2 0.0 all-gather.8.cloned.1.call-start
  84.3 0.8 dynamic-slice_convert_fusion.1
  85.1 80.1 %all-gather.6.cloned.1.call-done = bf16[512,4096]{1,0:T(8,128)(2,1)} async-done(((bf16[512,1024]{1,0:T(8,128)(2,1)}), bf16[512,4096]{1,0:T(8,128)(2,1)}) %all-gather.6.cloned.1.call-update) | async-done | bytes 4194320 | tf_op jit(solution)/shard_map/all_gather | solution.py:39
  165.1 0.2 broadcast_in_dim.15
  165.3 10.9 %fusion.1 = (bf16[512,1024]{1,0:T(8,128)(2,1)}, f32[512,1024]{1,0:T(8,128)}) fusion(f32[64,8,8,128]{3,2,1,0:T(8,128)S(1)} %bitcast.24, bf16[512,4096]{1,0:T(8,128)(2,1)} %all-gather.6.cloned.1.call-done, bf16[4096,1024]{1,0:T(8,128)(2,1)} %copy-done.1), kind=kOutput, calls=%fused_computation.6 | convolution fusion | flops 4296015872 | bytes 17825792 | tf_op jit(solution)/shard_map/dot_general | solution.py:10
  176.3 0.0 all-gather.8.cloned.1.call-update
  176.3 79.4 %all-gather.8.cloned.1.call-done = bf16[512,4096]{1,0:T(8,128)(2,1)} async-done(((bf16[512,1024]{1,0:T(8,128)(2,1)}), bf16[512,4096]{1,0:T(8,128)(2,1)}) %all-gather.8.cloned.1.call-update) | async-done | bytes 4194320 | tf_op jit(solution)/shard_map/all_gather | solution.py:41
  255.7 10.9 %fusion = bf16[512,1024]{1,0:T(8,128)(2,1)} fusion(f32[64,8,8,128]{3,2,1,0:T(8,128)S(1)} %bitcast.25, f32[512,1024]{1,0:T(8,128)} %get-tuple-element.6, bf16[512,4096]{1,0:T(8,128)(2,1)} %all-gather.8.cloned.1.call-done, bf16[4096,1024]{1,0:T(8,128)(2,1)} %copy-done.1), kind=kOutput, calls=%fused_computation.5 | convolution fusion | flops 4298113024 | bytes 17825792 | tf_op jit(solution)/shard_map/dot_general | solution.py:10
  (3 shorter events, 0.0 us)
Async XLA Ops:
  6.5 59.7 %all-gather.4.cloned.1.call-start = ((), (), s32[]{:S(2)}) async-start(), calls=%async_computation | async-start | bytes 9437184 | tf_op jit(solution)/shard_map/all_gather | solution.py:19
  7.3 157.9 %all-gather.6.cloned.1.call-start = ((), (), s32[]{:S(2)}) async-start(), calls=%async_computation.1 | async-start | bytes 5242880 | tf_op jit(solution)/shard_map/all_gather | solution.py:39
  74.6 3.4 %copy-start = (bf16[32,128,1024]{2,1,0:T(8,128)(2,1)S(1)}, bf16[32,128,1024]{2,1,0:T(8,128)(2,1)}, u32[]{:S(2)}) copy-start(bf16[32,128,1024]{2,1,0:T(8,128)(2,1)} %gather_fusion) | copy-start | bytes 25165828
  79.9 3.2 %copy-start.1 = (bf16[4096,1024]{1,0:T(8,128)(2,1)}, bf16[4096,1024]{1,0:T(8,128)(2,1)S(1)}, u32[]{:S(2)}) copy-start(bf16[4096,1024]{1,0:T(8,128)(2,1)S(1)} %bitcast_multiply_fusion) | copy-start | bytes 25165828
  84.2 171.4 %all-gather.8.cloned.1.call-start = ((), (), s32[]{:S(2)}) async-start(), calls=%async_computation.2 | async-start | bytes 5242880 | tf_op jit(solution)/shard_map/all_gather | solution.py:41
Sparse Core Ops, SparseCore 0:
  9.2 56.9 all-gather.3
  84.4 80.7 all-gather.5
  176.4 79.2 all-gather.7
where the time goes:
time: 273 us
  waiting for transfers between devices  217 us (79%)
  matrix products  21.8 us (8%)
  local copies, waits for them, and re-layouts  16.9 us (6%)
  between operations  13.2 us (5%)
  other arithmetic  4.14 us (2%)
    all_gather x1, waiting for transfers between devices, body(): lax.all_gather(local_tile, 'col', axis=1, tiled=True)  80.1 us
    all_gather x1, waiting for transfers between devices, body(): lax.all_gather(rounded, 'col', axis=1, tiled=True)  79.4 us
    all_gather x1, waiting for transfers between devices, body(): build_slab = lax.all_gather(built, 'row', axis=0, tiled=True)  56.8 us
    dot_general x2, matrix products, contract(): return jnp.dot(portion, col_panel, preferred_element_type=jnp.float32)  21.8 us
    gather x1, local copies, waits for them, and re-layouts, body(): ordered = blocks[inverse].reshape(block_count, BS, col_count, BS)  8.42 us
  transfers between devices with their start and end apart: 3, of which 3 were waited for; matrix products, arithmetic and copies ran while one was open for 1% of the time, Pallas kernels for 0%

commit v1 on v0

v1 whole, which is shorter than its diff:
```python
import functools

import jax
import jax.numpy as jnp
from jax import lax
from jax.experimental import pallas as pl
from jax.experimental.pallas import tpu as pltpu
from jax.sharding import PartitionSpec as P

BS = 128
MESH = pl.DeviceIdType.MESH
BF = jnp.bfloat16
F32 = jnp.float32


def pack(dims, order, built, packed, inv):
    rows, cols, nr, nc = dims
    nb = rows * nr
    fold = nb // 2
    ways = packed.shape[0]
    first = (lax.axis_index("col") * nc) % fold
    for a in range(nr):
        f = lax.rem(order[lax.axis_index("row") * nr + a], fold)
        for s in range(3):
            q = lax.rem(f + (s - 1) + fold, fold) - first
            at = jnp.clip(q, 0, nc - 1) * BS
            block = built[a * BS : (a + 1) * BS, pl.ds(pl.multiple_of(at, BS), BS)]
            packed[:, a, s] = block.reshape(ways, BS // ways, BS)
    for b in range(nb):
        inv[order[b]] = b


def kernel(
    dims,
    inv,
    p_pat,
    q_pat,
    send1,
    out,
    recv1,
    send2,
    den,
    sib,
    sqf,
    sqr,
    sibq,
    res,
    s1,
    r1,
    s2,
    r2,
    s3,
    r3,
    s4,
    r4,
):
    rows, cols, nr, nc = dims
    nb = rows * nr
    fold = nb // 2
    ways = send1.shape[0]
    piece = BS // ways
    row = lax.axis_index("row")
    col = lax.axis_index("col")

    def place(k, h):
        back = k // (fold // 2)
        kk = k + back * (fold - 1 - 2 * k)
        z = kk // 2
        y = (kk + z) % 2
        return ((y * 2 + back) * 2 + h, z)

    barrier = pltpu.get_barrier_semaphore()
    me = row * cols + col

    def greet(j, carry):
        other = (me + j) % (rows * cols)
        pl.semaphore_signal(
            barrier, inc=1, device_id=(other // cols, other % cols), device_id_type=MESH
        )
        return carry

    out[...] = jnp.zeros_like(out)
    lax.fori_loop(1, rows * cols, greet, 0)

    first = (col * nc) % fold
    pl.semaphore_wait(barrier, rows * cols - 1)

    def copy1(t):
        return pltpu.make_async_remote_copy(
            src_ref=send1.at[t],
            dst_ref=recv1.at[pl.ds(row * nr, nr)],
            send_sem=s1.at[t],
            recv_sem=r1,
            device_id=(t, col),
            device_id_type=MESH,
        )

    def local1(t):
        return pltpu.make_async_copy(send1.at[t], recv1.at[pl.ds(row * nr, nr)], r1)

    for j in range(ways):
        t = (row + j) % ways

        @pl.when(t != row)
        def _():
            copy1(t).start()

        @pl.when(t == row)
        def _():
            local1(t).start()

    half = (col * nc) // fold

    def copy2(n):
        q, e = n // 3, n % 3
        l = (first + q + e - 1 + fold) % fold
        return place(l, half), pltpu.make_async_remote_copy(
            src_ref=send2.at[n],
            dst_ref=den.at[2, 2 - e, :, pl.ds(pl.multiple_of(row * piece, piece), piece)],
            send_sem=s2.at[n],
            recv_sem=r2,
            device_id=place(l, half),
            device_id_type=MESH,
        ), pltpu.make_async_copy(
            send2.at[n],
            den.at[2, 2 - e, :, pl.ds(pl.multiple_of(row * piece, piece), piece)],
            r2,
        )

    @pl.when(row < ways)
    def _():
        pltpu.make_async_copy(recv1, recv1, r1).wait()
        for n in range(3 * nc):
            q, e = n // 3, n % 3
            l = lax.rem(first + (q + e - 1) + fold, fold)
            for g in range(2):
                i = l + g * fold
                keep = p_pat[i, col * nc + q].astype(F32)
                send2[n, g] = (recv1[inv[i], 2 - e].astype(F32) * keep).astype(BF)

        def go(n, carry):
            dev, remote, local = copy2(n)
            mine = jnp.logical_and(dev[0] == row, dev[1] == col)

            @pl.when(jnp.logical_not(mine))
            def _():
                remote.start()

            @pl.when(mine)
            def _():
                local.start()

            return carry

        lax.fori_loop(0, 3 * nc, go, 0)

    m = row // 2
    h = row % 2
    kk = 2 * col + (m // 2 + col) % 2
    k = kk + (m % 2) * (fold - 1 - 2 * kk)
    other = (row + 1 - 2 * h, col)

    def halo(j, d, lo, count):
        return pltpu.make_async_remote_copy(
            src_ref=den.at[2, pl.ds(lo, count)],
            dst_ref=den.at[2 - d, pl.ds(lo, count)],
            send_sem=s3.at[j],
            recv_sem=r3.at[j],
            device_id=place((k + d + fold) % fold, h),
            device_id_type=MESH,
        )

    def to_sib(j, src, dst):
        return pltpu.make_async_remote_copy(
            src_ref=src,
            dst_ref=dst,
            send_sem=s3.at[j],
            recv_sem=r3.at[j],
            device_id=other,
            device_id_type=MESH,
        )

    def copy4(n):
        d, g = n // 2, n % 2
        i = k + g * fold
        q = (k + d - 2 + fold) % fold
        j = q + h * fold
        dev = (i // nr, j // nc)
        a, b = i % nr, j % nc
        dst = out.at[
            pl.ds(pl.multiple_of(a * BS, BS), BS), pl.ds(pl.multiple_of(b * BS, BS), BS)
        ]
        sem = r4.at[a * nc + b]
        return dev, pltpu.make_async_remote_copy(
            src_ref=res.at[n],
            dst_ref=dst,
            send_sem=s4.at[n],
            recv_sem=sem,
            device_id=dev,
            device_id_type=MESH,
        ), pltpu.make_async_copy(res.at[n], dst, sem)

    @pl.when(m < 4)
    def _():
        pltpu.make_async_copy(den.at[2], den.at[2], r2).wait()
        sends = [
            to_sib(4, den.at[2], sib),
            halo(0, 1, 0, 3),
            halo(1, -1, 0, 3),
            halo(2, 2, 1, 2),
            halo(3, -2, 0, 2),
        ]
        for c in sends:
            c.start()

        def pair(mine, theirs):
            low = jnp.where(h == 0, mine.astype(F32), theirs.astype(F32)).astype(BF)
            high = jnp.where(h == 0, theirs.astype(F32), mine.astype(F32)).astype(BF)
            return jnp.concatenate([low, high], axis=1)

        def right(d, s):
            return den[2 + d, s].reshape(2 * BS, BS)

        def q_mask(d, g):
            q = (k + d + fold) % fold
            return q_pat[k + g * fold, q + h * fold].astype(F32)

        sends[0].wait_recv()
        sends[1].wait_recv()
        sends[2].wait_recv()
        left = [pair(right(0, s), sib[s].reshape(2 * BS, BS)) for s in range(3)]
        for d in range(-2, 3):
            total = None
            for l in range(-1, 2):
                if abs(d - l) <= 1:
                    term = jnp.dot(left[l + 1], right(l, d - l + 1), preferred_element_type=F32)
                    total = term if total is None else total + term
            for g in range(2):
                part = total[g * BS : (g + 1) * BS] * q_mask(d, g)
                sqf[d + 2, g * BS : (g + 1) * BS] = part
                sqr[d + 2, g * BS : (g + 1) * BS] = part.astype(BF)
        swap = to_sib(5, sqr, sibq)
        swap.start()
        sends[3].wait_recv()
        sends[4].wait_recv()
        swap.wait_recv()
        left2 = [pair(sqr[d], sibq[d]) for d in range(5)]
        for d in range(-2, 3):
            total = None
            for l in range(-2, 3):
                if abs(d - l) <= 1:
                    term = jnp.dot(left2[l + 2], right(l, d - l + 1), preferred_element_type=F32)
                    total = term if total is None else total + term
            for g in range(2):
                part = slice(g * BS, (g + 1) * BS)
                value = (3.0 * sqf[d + 2, part] - 2.0 * total[part]) * q_mask(d, g)
                res[2 * (d + 2) + g] = value.astype(BF)

        def go4(n, carry):
            dev, remote, local = copy4(n)
            mine = jnp.logical_and(dev[0] == row, dev[1] == col)

            @pl.when(jnp.logical_not(mine))
            def _():
                remote.start()

            @pl.when(mine)
            def _():
                local.start()

            return carry

        lax.fori_loop(0, 10, go4, 0)
        for c in sends:
            c.wait_send()
        swap.wait_send()

    def take(n, carry):
        a, b = n // nc, n % nc
        apart = (row * nr + a - col * nc - b + 2 + 2 * nb) % fold

        @pl.when(apart <= 4)
        def _():
            dst = out.at[
                pl.ds(pl.multiple_of(a * BS, BS), BS), pl.ds(pl.multiple_of(b * BS, BS), BS)
            ]
            pltpu.make_async_copy(dst, dst, r4.at[n]).wait()

        return carry

    lax.fori_loop(0, nr * nc, take, 0)

    for j in range(ways):
        t = (row + j) % ways

        @pl.when(t != row)
        def _():
            copy1(t).wait_send()

    @pl.when(row < ways)
    def _():
        def done(n, carry):
            dev, remote, _ = copy2(n)

            @pl.when(jnp.logical_not(jnp.logical_and(dev[0] == row, dev[1] == col)))
            def _():
                remote.wait_send()

            return carry

        lax.fori_loop(0, 3 * nc, done, 0)

    @pl.when(m < 4)
    def _():
        def done4(n, carry):
            dev, remote, _ = copy4(n)

            @pl.when(jnp.logical_not(jnp.logical_and(dev[0] == row, dev[1] == col)))
            def _():
                remote.wait_send()

            return carry

        lax.fori_loop(0, 10, done4, 0)


def body(rows, cols, built, build_order, p_pattern, q_pattern):
    nr = built.shape[0] // BS
    nc = built.shape[1] // BS
    nb = rows * nr
    ways = min(rows, 8)
    piece = BS // ways
    smem = pl.BlockSpec(memory_space=pltpu.SMEM)
    vmem = pl.BlockSpec(memory_space=pltpu.VMEM)
    dma = pltpu.SemaphoreType.DMA
    dims = (rows, cols, nr, nc)
    packed, inverse = pl.pallas_call(
        functools.partial(pack, dims),
        out_shape=(
            jax.ShapeDtypeStruct((ways, nr, 3, piece, BS), BF),
            jax.ShapeDtypeStruct((nb,), jnp.int32),
        ),
        in_specs=[smem, vmem],
        out_specs=(vmem, smem),
    )(build_order, built)
    return pl.pallas_call(
        functools.partial(kernel, dims),
        out_shape=jax.ShapeDtypeStruct(built.shape, BF),
        in_specs=[smem, smem, smem, vmem],
        out_specs=vmem,
        scratch_shapes=[
            pltpu.VMEM((nb, 3, piece, BS), BF),
            pltpu.VMEM((3 * nc, 2, piece, BS), BF),
            pltpu.VMEM((5, 3, 2, BS, BS), BF),
            pltpu.VMEM((3, 2, BS, BS), BF),
            pltpu.VMEM((5, 2 * BS, BS), F32),
            pltpu.VMEM((5, 2 * BS, BS), BF),
            pltpu.VMEM((5, 2 * BS, BS), BF),
            pltpu.VMEM((10, BS, BS), BF),
            dma((ways,)),
            dma,
            dma((3 * nc,)),
            dma,
            dma((6,)),
            dma((6,)),
            dma((10,)),
            dma((nr * nc,)),
        ],
        compiler_params=pltpu.CompilerParams(collective_id=0, has_side_effects=True),
    )(inverse, p_pattern, q_pattern, packed)


def solution(mesh):
    placed = (P("row", "col"), P(), P(), P())
    run = functools.partial(body, mesh.shape["row"], mesh.shape["col"])
    return jax.shard_map(
        run, mesh=mesh, in_specs=placed, out_specs=P("row", "col"), check_vma=False
    )
```

time: 273 us -> 52.1 us (0.19)
  waiting for transfers between devices: 217 us -> 0 us
  Pallas kernels: 0 us -> 49.6 us
  matrix products: 21.8 us -> 0 us
  local copies, waits for them, and re-layouts: 16.9 us -> 2.26 us
  between operations: 13.2 us -> 0.02 us
  other arithmetic: 4.14 us -> 0 us
    all_gather x3 -> x0, waiting for transfers between devices: 216 us -> none  [the longest x1 80.1 us: body(): lax.all_gather(local_tile, 'col', axis=1, tiled=True)]
    pallas_call x0 -> x2, Pallas kernels: none -> 49.6 us  [the longest x1 47.5 us: body(): pl.pallas_call(functools.partial(kernel, dims), out_shape=jax.ShapeDtypeS...]
    dot_general x2 -> x0, matrix products: 21.8 us -> none  [contract(): return jnp.dot(portion, col_panel, preferred_element_type=jnp.float32)]
    gather x1 -> x0, local copies, waits for them, and re-layouts: 8.42 us -> none  [body(): ordered = blocks[inverse].reshape(block_count, BS, col_count, BS)]
    unnamed x4 -> x1, local copies, waits for them, and re-layouts: 5.44 us -> 2.26 us
  transfers between devices with their start and end apart: 3 -> 0, of which waited for: 3 -> 0; matrix products, arithmetic and copies ran while one was open for 1% -> 0% of each run, Pallas kernels for 0% -> 0%
where the time goes in v1:
time: 52.1 us; the launch traced here: 51.9 us
  Pallas kernels  49.6 us (95%)
  local copies, waits for them, and re-layouts  2.26 us (4%)
    pallas_call x1, Pallas kernels, body(): pl.pallas_call(functools.partial(kernel, dims), out_shape=jax.ShapeDtypeS...  47.5 us
    unnamed x1, local copies, waits for them, and re-layouts  2.26 us
    pallas_call x1, Pallas kernels, body(): pl.pallas_call(functools.partial(pack, dims), out_shape=(jax.ShapeDtypeSt...  2.11 us

profile of v1, /device:TPU:0, one launch (start us, length us, event | category | flops | bytes accessed | tf_op | source)
XLA Modules:
  0.0 51.9 jit_solution(2718805163060279445)
XLA Ops:
  0.0 2.1 %shard_map.46 = (bf16[8,4,3,16,128]{4,3,2,1,0:T(8,128)(2,1)}, s32[32]{0:T(128)}) custom-call(s32[32]{0:T(128)} %order.1, bf16[512,1024]{1,0:T(8,128)(2,1)} %built.1), custom_call_target="tpu_custom_call" | custom-call | tf_op jit(solution)/shard_map/pallas_call | solution.py:337
  2.1 47.5 %shard_map.47 = bf16[512,1024]{1,0:T(8,128)(2,1)} custom-call(s32[32]{0:T(128)} %get-tuple-element.7.inv, s32[32,32]{1,0:T(8,128)} %p_pat.1, s32[32,32]{1,0:T(8,128)} %q_pat.1, bf16[8,4,3,16,128]{4,3,2,1,0:T(8,128)(2,1)} %get-tuple-element.8.send1), custom_call_target="tpu_custom_call" | custom-call | tf_op jit(solution)/shard_map/pallas_call | solution.py:346
  49.6 2.3 %copy.6 = bf16[512,1024]{1,0:T(8,128)(2,1)} copy(bf16[512,1024]{1,0:T(8,128)(2,1)} %shard_map.47) | data formatting | bytes 2097152

commit v2 on v1

--- a/solution.py
+++ b/solution.py
@@ -53,6 +53,7 @@
     r3,
     s4,
     r4,
+    heard,
 ):
     rows, cols, nr, nc = dims
     nb = rows * nr
@@ -63,27 +64,35 @@
     col = lax.axis_index("col")
 
     def place(k, h):
-        back = k // (fold // 2)
-        kk = k + back * (fold - 1 - 2 * k)
-        z = kk // 2
-        y = (kk + z) % 2
-        return ((y * 2 + back) * 2 + h, z)
+        if cols != 4:
+            back = k // (fold // 2)
+            kk = k + back * (fold - 1 - 2 * k)
+            z = kk // 2
+            return ((((kk + z) % 2) * 2 + back) * 2 + h, z)
+        upper = k // 8
+        j = k + upper * (15 - 2 * k)
+        z = 1 - ((j + 1) // 2) % 2
+        return (((((j + 2) // 4) % 2) * 2 + j // 4) * 2 + h, z + upper * (3 - 2 * z))
 
     barrier = pltpu.get_barrier_semaphore()
-    me = row * cols + col
-
-    def greet(j, carry):
-        other = (me + j) % (rows * cols)
+
+    def greet_row(j, carry):
         pl.semaphore_signal(
-            barrier, inc=1, device_id=(other // cols, other % cols), device_id_type=MESH
+            barrier, inc=1, device_id=((row + j) % rows, col), device_id_type=MESH
         )
         return carry
 
+    def greet_col(sem, j, carry):
+        pl.semaphore_signal(sem, inc=1, device_id=(row, (col + j) % cols), device_id_type=MESH)
+        return carry
+
+    lax.fori_loop(1, cols, functools.partial(greet_col, barrier), 0)
+    lax.fori_loop(1, rows, greet_row, 0)
     out[...] = jnp.zeros_like(out)
-    lax.fori_loop(1, rows * cols, greet, 0)
 
     first = (col * nc) % fold
-    pl.semaphore_wait(barrier, rows * cols - 1)
+    pl.semaphore_wait(barrier, rows + cols - 2)
+    lax.fori_loop(1, cols, functools.partial(greet_col, heard), 0)
 
     def copy1(t):
         return pltpu.make_async_remote_copy(
@@ -109,34 +118,36 @@
         def _():
             local1(t).start()
 
+    pl.semaphore_wait(heard, cols - 1)
+
     half = (col * nc) // fold
 
     def copy2(n):
-        q, e = n // 3, n % 3
-        l = (first + q + e - 1 + fold) % fold
+        q, s = n % nc, (2 + n // nc) % 3
+        l = (first + q + 1 - s + fold) % fold
         return place(l, half), pltpu.make_async_remote_copy(
             src_ref=send2.at[n],
-            dst_ref=den.at[2, 2 - e, :, pl.ds(pl.multiple_of(row * piece, piece), piece)],
+            dst_ref=den.at[2, s, :, pl.ds(pl.multiple_of(row * piece, piece), piece)],
             send_sem=s2.at[n],
-            recv_sem=r2,
+            recv_sem=r2.at[s],
             device_id=place(l, half),
             device_id_type=MESH,
         ), pltpu.make_async_copy(
             send2.at[n],
-            den.at[2, 2 - e, :, pl.ds(pl.multiple_of(row * piece, piece), piece)],
-            r2,
+            den.at[2, s, :, pl.ds(pl.multiple_of(row * piece, piece), piece)],
+            r2.at[s],
         )
 
     @pl.when(row < ways)
     def _():
         pltpu.make_async_copy(recv1, recv1, r1).wait()
         for n in range(3 * nc):
-            q, e = n // 3, n % 3
-            l = lax.rem(first + (q + e - 1) + fold, fold)
+            q, s = n % nc, (2 + n // nc) % 3
+            l = lax.rem(first + (q + 1 - s) + fold, fold)
             for g in range(2):
                 i = l + g * fold
                 keep = p_pat[i, col * nc + q].astype(F32)
-                send2[n, g] = (recv1[inv[i], 2 - e].astype(F32) * keep).astype(BF)
+                send2[n, g] = (recv1[inv[i], s].astype(F32) * keep).astype(BF)
 
         def go(n, carry):
             dev, remote, local = copy2(n)
@@ -156,14 +167,22 @@
 
     m = row // 2
     h = row % 2
-    kk = 2 * col + (m // 2 + col) % 2
-    k = kk + (m % 2) * (fold - 1 - 2 * kk)
+    y, x = m // 2, m % 2
+    if cols != 4:
+        kk = 2 * col + (y + col) % 2
+        k = kk + x * (fold - 1 - 2 * kk)
+    else:
+        upper = col // 2
+        z = col + upper * (3 - 2 * col)
+        j = 1 - z + y * (1 + 2 * z)
+        j = j + x * (7 - 2 * j)
+        k = j + upper * (15 - 2 * j)
     other = (row + 1 - 2 * h, col)
 
-    def halo(j, d, lo, count):
+    def hop(j, d, far, s):
         return pltpu.make_async_remote_copy(
-            src_ref=den.at[2, pl.ds(lo, count)],
-            dst_ref=den.at[2 - d, pl.ds(lo, count)],
+            src_ref=den.at[2 - far * d, s],
+            dst_ref=den.at[2 - (far + 1) * d, s],
             send_sem=s3.at[j],
             recv_sem=r3.at[j],
             device_id=place((k + d + fold) % fold, h),
@@ -202,15 +221,21 @@
 
     @pl.when(m < 4)
     def _():
-        pltpu.make_async_copy(den.at[2], den.at[2], r2).wait()
-        sends = [
-            to_sib(4, den.at[2], sib),
-            halo(0, 1, 0, 3),
-            halo(1, -1, 0, 3),
-            halo(2, 2, 1, 2),
-            halo(3, -2, 0, 2),
-        ]
-        for c in sends:
+        near = {(d, s): hop(3 * i + s, d, 0, s) for i, d in enumerate((1, -1)) for s in range(3)}
+        relay = [((1, 2), hop(6, 1, 1, 2)), ((-1, 0), hop(7, -1, 1, 0))]
+        relay += [((1, 1), hop(8, 1, 1, 1)), ((-1, 1), hop(9, -1, 1, 1))]
+        given = to_sib(10, den.at[2], sib)
+        for s, starts in (
+            (2, [(1, 2)]),
+            (0, [(-1, 0)]),
+            (1, [(1, 1), (-1, 1), (1, 0), (-1, 2)]),
+        ):
+            pltpu.make_async_copy(den.at[2, s], den.at[2, s], r2.at[s]).wait()
+            for key in starts:
+                near[key].start()
+        given.start()
+        for key, c in relay:
+            near[key].wait_recv()
             c.start()
 
         def pair(mine, theirs):
@@ -225,9 +250,9 @@
             q = (k + d + fold) % fold
             return q_pat[k + g * fold, q + h * fold].astype(F32)
 
-        sends[0].wait_recv()
-        sends[1].wait_recv()
-        sends[2].wait_recv()
+        near[1, 0].wait_recv()
+        near[-1, 2].wait_recv()
+        given.wait_recv()
         left = [pair(right(0, s), sib[s].reshape(2 * BS, BS)) for s in range(3)]
         for d in range(-2, 3):
             total = None
@@ -239,10 +264,10 @@
                 part = total[g * BS : (g + 1) * BS] * q_mask(d, g)
                 sqf[d + 2, g * BS : (g + 1) * BS] = part
                 sqr[d + 2, g * BS : (g + 1) * BS] = part.astype(BF)
-        swap = to_sib(5, sqr, sibq)
+        swap = to_sib(11, sqr, sibq)
         swap.start()
-        sends[3].wait_recv()
-        sends[4].wait_recv()
+        for _, c in relay:
+            c.wait_recv()
         swap.wait_recv()
         left2 = [pair(sqr[d], sibq[d]) for d in range(5)]
         for d in range(-2, 3):
@@ -271,7 +296,7 @@
             return carry
 
         lax.fori_loop(0, 10, go4, 0)
-        for c in sends:
+        for c in [*near.values(), *[c for _, c in relay], given]:
             c.wait_send()
         swap.wait_send()
 
@@ -360,11 +385,12 @@
             dma((ways,)),
             dma,
             dma((3 * nc,)),
-            dma,
-            dma((6,)),
-            dma((6,)),
+            dma((3,)),
+            dma((12,)),
+            dma((12,)),
             dma((10,)),
             dma((nr * nc,)),
+            pltpu.SemaphoreType.REGULAR,
         ],
         compiler_params=pltpu.CompilerParams(collective_id=0, has_side_effects=True),
     )(inverse, p_pattern, q_pattern, packed)

time: 52.1 us -> 44.8 us (0.86)
  Pallas kernels: 49.6 us -> 42.3 us
    pallas_call x1, Pallas kernels: 47.5 us -> 40.2 us  [body(): pl.pallas_call(functools.partial(kernel, dims), out_shape=jax.ShapeDtypeS...]
where the time goes in v2:
time: 44.8 us; the launch traced here: 44.6 us
  Pallas kernels  42.3 us (94%)
  local copies, waits for them, and re-layouts  2.26 us (5%)
    pallas_call x1, Pallas kernels, body(): pl.pallas_call(functools.partial(kernel, dims), out_shape=jax.ShapeDtypeS...  40.2 us
    unnamed x1, local copies, waits for them, and re-layouts  2.26 us
    pallas_call x1, Pallas kernels, body(): pl.pallas_call(functools.partial(pack, dims), out_shape=(jax.ShapeDtypeSt...  2.11 us

profile of v2, /device:TPU:0, one launch (start us, length us, event | category | flops | bytes accessed | tf_op | source)
XLA Modules:
  0.0 44.6 jit_solution(13480768946689346927)
XLA Ops:
  0.0 2.1 %shard_map.46 = (bf16[8,4,3,16,128]{4,3,2,1,0:T(8,128)(2,1)}, s32[32]{0:T(128)}) custom-call(s32[32]{0:T(128)} %order.1, bf16[512,1024]{1,0:T(8,128)(2,1)} %built.1), custom_call_target="tpu_custom_call" | custom-call | tf_op jit(solution)/shard_map/pallas_call | solution.py:362
  2.1 40.2 %shard_map.47 = bf16[512,1024]{1,0:T(8,128)(2,1)} custom-call(s32[32]{0:T(128)} %get-tuple-element.7.inv, s32[32,32]{1,0:T(8,128)} %p_pat.1, s32[32,32]{1,0:T(8,128)} %q_pat.1, bf16[8,4,3,16,128]{4,3,2,1,0:T(8,128)(2,1)} %get-tuple-element.8.send1), custom_call_target="tpu_custom_call" | custom-call | tf_op jit(solution)/shard_map/pallas_call | solution.py:371
  42.4 2.3 %copy.6 = bf16[512,1024]{1,0:T(8,128)(2,1)} copy(bf16[512,1024]{1,0:T(8,128)(2,1)} %shard_map.47) | data formatting | bytes 2097152

commit v3 on v2

--- a/solution.py
+++ b/solution.py
@@ -13,30 +13,20 @@
 F32 = jnp.float32
 
 
-def pack(dims, order, built, packed, inv):
-    rows, cols, nr, nc = dims
-    nb = rows * nr
-    fold = nb // 2
-    ways = packed.shape[0]
-    first = (lax.axis_index("col") * nc) % fold
-    for a in range(nr):
-        f = lax.rem(order[lax.axis_index("row") * nr + a], fold)
-        for s in range(3):
-            q = lax.rem(f + (s - 1) + fold, fold) - first
-            at = jnp.clip(q, 0, nc - 1) * BS
-            block = built[a * BS : (a + 1) * BS, pl.ds(pl.multiple_of(at, BS), BS)]
-            packed[:, a, s] = block.reshape(ways, BS // ways, BS)
-    for b in range(nb):
-        inv[order[b]] = b
-
-
 def kernel(
     dims,
-    inv,
+    order_hbm,
+    p_hbm,
+    q_hbm,
+    built_hbm,
+    out,
+    order,
     p_pat,
     q_pat,
+    built,
+    s0,
+    inv,
     send1,
-    out,
     recv1,
     send2,
     den,
@@ -74,6 +64,20 @@
         z = 1 - ((j + 1) // 2) % 2
         return (((((j + 2) // 4) % 2) * 2 + j // 4) * 2 + h, z + upper * (3 - 2 * z))
 
+    loads = [
+        pltpu.make_async_copy(order_hbm, order, s0.at[nr]),
+        *[
+            pltpu.make_async_copy(
+                built_hbm.at[pl.ds(a * BS, BS)], built.at[pl.ds(a * BS, BS)], s0.at[a]
+            )
+            for a in range(nr)
+        ],
+        pltpu.make_async_copy(p_hbm, p_pat, s0.at[nr + 1]),
+        pltpu.make_async_copy(q_hbm, q_pat, s0.at[nr + 2]),
+    ]
+    for c in loads:
+        c.start()
+
     barrier = pltpu.get_barrier_semaphore()
 
     def greet_row(j, carry):
@@ -91,6 +95,18 @@
     out[...] = jnp.zeros_like(out)
 
     first = (col * nc) % fold
+    loads[0].wait()
+    for a in range(nr):
+        loads[1 + a].wait()
+        f = lax.rem(order[row * nr + a], fold)
+        for s in range(3):
+            q = lax.rem(f + (s - 1) + fold, fold) - first
+            block = built[a * BS : (a + 1) * BS, :BS]
+            for c in range(1, nc):
+                here = built[a * BS : (a + 1) * BS, c * BS : (c + 1) * BS]
+                block = jnp.where(q == c, here, block)
+            send1[:, a, s] = block.reshape(ways, piece, BS)
+
     pl.semaphore_wait(barrier, rows + cols - 2)
     lax.fori_loop(1, cols, functools.partial(greet_col, heard), 0)
 
@@ -118,7 +134,17 @@
         def _():
             local1(t).start()
 
+    def invert(i, carry):
+        v = 0
+        for b in range(nb):
+            v = jnp.maximum(v, (order[b] == i).astype(jnp.int32) * b)
+        inv[i] = v
+        return carry
+
+    lax.fori_loop(0, nb, invert, 0)
     pl.semaphore_wait(heard, cols - 1)
+    loads[nr + 1].wait()
+    loads[nr + 2].wait()
 
     half = (col * nc) // fold
 
@@ -355,25 +381,23 @@
     nb = rows * nr
     ways = min(rows, 8)
     piece = BS // ways
-    smem = pl.BlockSpec(memory_space=pltpu.SMEM)
+    hbm = pl.BlockSpec(memory_space=pltpu.HBM)
     vmem = pl.BlockSpec(memory_space=pltpu.VMEM)
     dma = pltpu.SemaphoreType.DMA
     dims = (rows, cols, nr, nc)
-    packed, inverse = pl.pallas_call(
-        functools.partial(pack, dims),
-        out_shape=(
-            jax.ShapeDtypeStruct((ways, nr, 3, piece, BS), BF),
-            jax.ShapeDtypeStruct((nb,), jnp.int32),
-        ),
-        in_specs=[smem, vmem],
-        out_specs=(vmem, smem),
-    )(build_order, built)
     return pl.pallas_call(
         functools.partial(kernel, dims),
         out_shape=jax.ShapeDtypeStruct(built.shape, BF),
-        in_specs=[smem, smem, smem, vmem],
+        in_specs=[hbm] * 4,
         out_specs=vmem,
         scratch_shapes=[
+            pltpu.SMEM((nb,), jnp.int32),
+            pltpu.SMEM((nb, nb), jnp.int32),
+            pltpu.SMEM((nb, nb), jnp.int32),
+            pltpu.VMEM(built.shape, BF),
+            dma((nr + 3,)),
+            pltpu.SMEM((nb,), jnp.int32),
+            pltpu.VMEM((ways, nr, 3, piece, BS), BF),
             pltpu.VMEM((nb, 3, piece, BS), BF),
             pltpu.VMEM((3 * nc, 2, piece, BS), BF),
             pltpu.VMEM((5, 3, 2, BS, BS), BF),
@@ -392,8 +416,8 @@
             dma((nr * nc,)),
             pltpu.SemaphoreType.REGULAR,
         ],
-        compiler_params=pltpu.CompilerParams(collective_id=0, has_side_effects=True),
-    )(inverse, p_pattern, q_pattern, packed)
+        compiler_params=pltpu.CompilerParams(collective_id=0, has_side_effects=True, vmem_limit_bytes=16 * 1024 * 1024),
+    )(*[pltpu.with_memory_space_constraint(x, pltpu.HBM) for x in (build_order, p_pattern, q_pattern, built)])
 
 
 def solution(mesh):

time: 44.8 us -> 39.2 us (0.88)
  Pallas kernels: 42.3 us -> 38.1 us
  local copies, waits for them, and re-layouts: 2.26 us -> 0.97 us
    pallas_call x1, Pallas kernels: 40.2 us -> 38.1 us  [body(): pl.pallas_call(functools.partial(kernel, dims), out_shape=jax.ShapeDtypeS...]
    pallas_call x1 -> x0, Pallas kernels: 2.11 us -> none  [body(): pl.pallas_call(functools.partial(pack, dims), out_shape=(jax.ShapeDtypeSt...]
    unnamed x1, local copies, waits for them, and re-layouts: 2.26 us -> 0.97 us
where the time goes in v3:
time: 39.2 us; the launch traced here: 39.1 us
  Pallas kernels  38.1 us (97%)
  local copies, waits for them, and re-layouts  0.97 us (2%)
    pallas_call x1, Pallas kernels, body(): pl.pallas_call(functools.partial(kernel, dims), out_shape=jax.ShapeDtypeS...  38.1 us
    unnamed x1, local copies, waits for them, and re-layouts  0.97 us

profile of v3, /device:TPU:0, one launch (start us, length us, event | category | flops | bytes accessed | tf_op | source)
XLA Modules:
  0.0 39.1 jit_solution(5407354313349191819)
XLA Ops:
  0.0 38.1 %shard_map.46 = bf16[512,1024]{1,0:T(8,128)(2,1)S(1)} custom-call(s32[32]{0:T(128)} %order_hbm.1, s32[32,32]{1,0:T(8,128)} %p_hbm.1, s32[32,32]{1,0:T(8,128)} %q_hbm.1, bf16[512,1024]{1,0:T(8,128)(2,1)} %built_hbm.1), custom_call_target="tpu_custom_call" | custom-call | tf_op jit(solution)/shard_map/pallas_call | solution.py:388
  38.1 1.0 %copy.6 = bf16[512,1024]{1,0:T(8,128)(2,1)} copy(bf16[512,1024]{1,0:T(8,128)(2,1)S(1)} %shard_map.46) | data formatting | bytes 2097152

commit v4 on v3

--- a/solution.py
+++ b/solution.py
@@ -280,7 +280,9 @@
         near[-1, 2].wait_recv()
         given.wait_recv()
         left = [pair(right(0, s), sib[s].reshape(2 * BS, BS)) for s in range(3)]
-        for d in range(-2, 3):
+        swaps = [to_sib(11 + d, sqr.at[d], sibq.at[d]) for d in range(5)]
+        turn = (0, 1, -1, 2, -2)
+        for step, d in enumerate(turn):
             total = None
             for l in range(-1, 2):
                 if abs(d - l) <= 1:
@@ -290,41 +292,52 @@
                 part = total[g * BS : (g + 1) * BS] * q_mask(d, g)
                 sqf[d + 2, g * BS : (g + 1) * BS] = part
                 sqr[d + 2, g * BS : (g + 1) * BS] = part.astype(BF)
-        swap = to_sib(11, sqr, sibq)
-        swap.start()
-        for _, c in relay:
-            c.wait_recv()
-        swap.wait_recv()
-        left2 = [pair(sqr[d], sibq[d]) for d in range(5)]
-        for d in range(-2, 3):
+            if step:
+                swaps[turn[step - 1] + 2].start()
+        swaps[turn[-1] + 2].start()
+
+        def go4(n):
+            dev, remote, local = copy4(n)
+            mine = jnp.logical_and(dev[0] == row, dev[1] == col)
+
+            @pl.when(jnp.logical_not(mine))
+            def _():
+                remote.start()
+
+            @pl.when(mine)
+            def _():
+                local.start()
+
+        left2 = {}
+
+        def rounded_pair(l):
+            if l not in left2:
+                swaps[l + 2].wait_recv()
+                left2[l] = pair(sqr[l + 2], sibq[l + 2])
+            return left2[l]
+
+        needs = {1: relay[1][1], -1: relay[0][1], 2: relay[3][1], -2: relay[2][1]}
+        for step, d in enumerate(turn):
+            if d in needs:
+                needs[d].wait_recv()
             total = None
             for l in range(-2, 3):
                 if abs(d - l) <= 1:
-                    term = jnp.dot(left2[l + 2], right(l, d - l + 1), preferred_element_type=F32)
+                    term = jnp.dot(rounded_pair(l), right(l, d - l + 1), preferred_element_type=F32)
                     total = term if total is None else total + term
             for g in range(2):
                 part = slice(g * BS, (g + 1) * BS)
                 value = (3.0 * sqf[d + 2, part] - 2.0 * total[part]) * q_mask(d, g)
                 res[2 * (d + 2) + g] = value.astype(BF)
-
-        def go4(n, carry):
-            dev, remote, local = copy4(n)
-            mine = jnp.logical_and(dev[0] == row, dev[1] == col)
-
-            @pl.when(jnp.logical_not(mine))
-            def _():
-                remote.start()
-
-            @pl.when(mine)
-            def _():
-                local.start()
-
-            return carry
-
-        lax.fori_loop(0, 10, go4, 0)
+            if step:
+                go4(2 * (turn[step - 1] + 2))
+                go4(2 * (turn[step - 1] + 2) + 1)
+        go4(2 * (turn[-1] + 2))
+        go4(2 * (turn[-1] + 2) + 1)
         for c in [*near.values(), *[c for _, c in relay], given]:
             c.wait_send()
-        swap.wait_send()
+        for c in swaps:
+            c.wait_send()
 
     def take(n, carry):
         a, b = n // nc, n % nc
@@ -410,8 +423,8 @@
             dma,
             dma((3 * nc,)),
             dma((3,)),
-            dma((12,)),
-            dma((12,)),
+            dma((16,)),
+            dma((16,)),
             dma((10,)),
             dma((nr * nc,)),
             pltpu.SemaphoreType.REGULAR,

time: 39.2 us -> 38.8 us (0.990)
  Pallas kernels: 38.1 us -> 37.7 us
    pallas_call x1, Pallas kernels: 38.1 us -> 37.7 us  [body(): pl.pallas_call(functools.partial(kernel, dims), out_shape=jax.ShapeDtypeS...]
where the time goes in v4:
time: 38.8 us; the launch traced here: 38.6 us
  Pallas kernels  37.7 us (97%)
  local copies, waits for them, and re-layouts  0.97 us (2%)
    pallas_call x1, Pallas kernels, body(): pl.pallas_call(functools.partial(kernel, dims), out_shape=jax.ShapeDtypeS...  37.7 us
    unnamed x1, local copies, waits for them, and re-layouts  0.97 us

profile of v4, /device:TPU:0, one launch (start us, length us, event | category | flops | bytes accessed | tf_op | source)
XLA Modules:
  0.0 38.6 jit_solution(2332479611097751673)
XLA Ops:
  0.0 37.7 %shard_map.46 = bf16[512,1024]{1,0:T(8,128)(2,1)S(1)} custom-call(s32[32]{0:T(128)} %order_hbm.1, s32[32,32]{1,0:T(8,128)} %p_hbm.1, s32[32,32]{1,0:T(8,128)} %q_hbm.1, bf16[512,1024]{1,0:T(8,128)(2,1)} %built_hbm.1), custom_call_target="tpu_custom_call" | custom-call | tf_op jit(solution)/shard_map/pallas_call | solution.py:401
  37.7 1.0 %copy.6 = bf16[512,1024]{1,0:T(8,128)(2,1)} copy(bf16[512,1024]{1,0:T(8,128)(2,1)S(1)} %shard_map.46) | data formatting | bytes 2097152

commit v5 on v4

--- a/solution.py
+++ b/solution.py
@@ -167,6 +167,20 @@
     @pl.when(row < ways)
     def _():
         pltpu.make_async_copy(recv1, recv1, r1).wait()
+        def go(n, carry):
+            dev, remote, local = copy2(n)
+            mine = jnp.logical_and(dev[0] == row, dev[1] == col)
+
+            @pl.when(jnp.logical_not(mine))
+            def _():
+                remote.start()
+
+            @pl.when(mine)
+            def _():
+                local.start()
+
+            return carry
+
         for n in range(3 * nc):
             q, s = n % nc, (2 + n // nc) % 3
             l = lax.rem(first + (q + 1 - s) + fold, fold)
@@ -174,22 +188,10 @@
                 i = l + g * fold
                 keep = p_pat[i, col * nc + q].astype(F32)
                 send2[n, g] = (recv1[inv[i], s].astype(F32) * keep).astype(BF)
-
-        def go(n, carry):
-            dev, remote, local = copy2(n)
-            mine = jnp.logical_and(dev[0] == row, dev[1] == col)
-
-            @pl.when(jnp.logical_not(mine))
-            def _():
-                remote.start()
-
-            @pl.when(mine)
-            def _():
-                local.start()
-
-            return carry
-
-        lax.fori_loop(0, 3 * nc, go, 0)
+            if n % nc == nc - 1 and n >= nc:
+                lax.fori_loop(n + 1 - 2 * nc, n + 1 - nc, go, 0)
+
+        lax.fori_loop(2 * nc, 3 * nc, go, 0)
 
     m = row // 2
     h = row % 2

time: 38.8 us -> 38.8 us (level)
  no operation moved by 1% of the time
where the time goes in v5:
time: 38.8 us; the launch traced here: 38.6 us
  Pallas kernels  37.6 us (97%)
  local copies, waits for them, and re-layouts  0.97 us (2%)
    pallas_call x1, Pallas kernels, body(): pl.pallas_call(functools.partial(kernel, dims), out_shape=jax.ShapeDtypeS...  37.6 us
    unnamed x1, local copies, waits for them, and re-layouts  0.97 us

profile of v5, /device:TPU:0, one launch (start us, length us, event | category | flops | bytes accessed | tf_op | source)
XLA Modules:
  0.0 38.6 jit_solution(8323574150606171669)
XLA Ops:
  0.0 37.6 %shard_map.46 = bf16[512,1024]{1,0:T(8,128)(2,1)S(1)} custom-call(s32[32]{0:T(128)} %order_hbm.1, s32[32,32]{1,0:T(8,128)} %p_hbm.1, s32[32,32]{1,0:T(8,128)} %q_hbm.1, bf16[512,1024]{1,0:T(8,128)(2,1)} %built_hbm.1), custom_call_target="tpu_custom_call" | custom-call | tf_op jit(solution)/shard_map/pallas_call | solution.py:403
  37.7 1.0 %copy.6 = bf16[512,1024]{1,0:T(8,128)(2,1)} copy(bf16[512,1024]{1,0:T(8,128)(2,1)S(1)} %shard_map.46) | data formatting | bytes 2097152
